TPU v7x, 128 devices: a whole 4x4x4 slice. The times are simulated.
128 devices in a mesh: req: 16 (over y, z), seq: 2 (over core), exp: 4 (over x).
Axes of the slice: x: 4, y: 4, z: 4, core: 2. Of those that a mesh axis runs over, the one named last changes fastest.
Arguments:
- residual: bfloat16 [256, 7168], P(('req', 'seq', 'exp')), may hold values from -6 to 6
- queries: bfloat16 [16, 16, 128, 576], P('req', None, 'exp'), may hold values from -60 to 60
- latent_cache: bfloat16 [16, 384, 576], P('req', 'seq'), may hold values from -20 to 20
- blocks: int32 [16, 2, 2], P('req', 'seq'), may hold values from 0 to 2, as said below
- lengths: int32 [16], P('req'), may hold values from 208 to 384, as said below
- value_up: bfloat16 [128, 512, 128], P('exp'), may hold values from -0.25 to 0.25
- out_proj: bfloat16 [16384, 7168], P('exp', ('req', 'seq')), may hold values from -0.046875 to 0.046875
- norm_gain: bfloat16 [7168], replicated, may hold values from 0.099609375 to 1.8984375
- router: bfloat16 [7168, 16], replicated, may hold values from -0.0625 to 0.0625
- expert_ids: int32 [256, 8], P(('req', 'seq', 'exp')), may hold values from 0 to 15, all different within a row; in each aligned block of 2 rows (0 to 1, 2 to 3, ...) at most 2 rows name the same one
- w_gate: bfloat16 [16, 7168, 2048], P('req', None, ('seq', 'exp')), may hold values from -0.0625 to 0.0625
- w_up: bfloat16 [16, 7168, 2048], P('req', None, ('seq', 'exp')), may hold values from -0.0625 to 0.0625
- w_down: bfloat16 [16, 2048, 7168], P('req', ('seq', 'exp')), may hold values from -0.125 to 0.125
Outputs:
- layer_out: bfloat16 [256, 7168], P(('req', 'seq', 'exp'))
Inputs may be any that keep to these rules, and one draw needn't show every extreme that they name: `blocks`: each request and shard lists 2 different block numbers of that shard. `lengths`: some request has exactly 384, some exactly 208. `expert_ids`: each row names 8 different experts; among the rows of one device (aligned blocks of 2 rows) no expert is named more than 2 times, a bound that some block reaches.
All inputs are finite; a program needn't handle non-finite values.
Results may differ from a plain program's by a relative error of at most 0.019.
Values may be sent and summed in bfloat16 or wider, within the bound.
No kernel may reach another device: no remote copies, remote signals or barrier semaphores. Data moves between devices by JAX's collectives and lax.ppermute only.
A program may use at most 128 MiB of HBM per device.

v0:
```python
import jax
import jax.numpy as jnp
from jax import lax
from jax.sharding import PartitionSpec as P

DL = 512
DR = 64
DV = 128
BLOCK = 64


def combined_all(x, axis, join):
    gathered = jax.tree.map(
        lambda a, kind: lax.all_gather(a.astype(kind), axis),
        x,
        (jnp.bfloat16, jnp.bfloat16, jnp.bfloat16),
    )

    def take(source):
        return jax.tree.map(
            lambda a, own: lax.dynamic_index_in_dim(a, source, 0, False).astype(own.dtype),
            gathered,
            x,
        )

    return lax.fori_loop(
        1, lax.axis_size(axis), lambda source, state: join(state, take(source)), take(0)
    )


def merge_parts(former, latter):
    row_max = jnp.maximum(former[0], latter[0])
    left_scale = jnp.exp(former[0] - row_max)
    right_scale = jnp.exp(latter[0] - row_max)
    return (
        row_max,
        left_scale * former[1] + right_scale * latter[1],
        left_scale[..., None] * former[2] + right_scale[..., None] * latter[2],
    )


def pick_rows(block_rows, picks):
    return block_rows[picks]


def shard_softmax(queries, picked, usable):
    scores = jnp.einsum("bqhk,bjk->bqhj", queries, picked, preferred_element_type=jnp.float32) * (
        DV + DR
    ) ** (-0.5)
    row_max = jnp.max(jnp.where(usable, scores, -1e30), axis=-1)
    weights = jnp.where(usable, jnp.exp(scores - row_max[..., None]), 0.0).astype(jnp.bfloat16)
    row_sum = jnp.sum(weights.astype(jnp.float32), -1)
    weighted = jnp.einsum(
        "bqhj,bjd->bqhd", weights, picked[..., :DL], preferred_element_type=jnp.float32
    )
    return (row_max, row_sum, weighted)


def expert_rows(arrived, w_gate, w_up, w_down):
    model_width = w_gate.shape[1]
    flat_rows = arrived.reshape(-1, model_width)
    gate_act = jnp.dot(flat_rows, w_gate[0], preferred_element_type=jnp.float32)
    up_act = jnp.dot(flat_rows, w_up[0], preferred_element_type=jnp.float32)
    activated = (jax.nn.silu(gate_act) * up_act).astype(jnp.bfloat16)
    partial_value = jnp.dot(activated, w_down[0], preferred_element_type=jnp.float32).astype(
        jnp.bfloat16
    )
    return partial_value.reshape(arrived.shape)


def per_device(
    residual,
    queries,
    latent_cache,
    blocks,
    lengths,
    value_up,
    out_proj,
    norm_gain,
    router,
    expert_ids,
    w_gate,
    w_up,
    w_down,
):
    local_reqs, drafts, head_count, qk_width = queries.shape
    shard_len = latent_cache.shape[1]
    picks_count = blocks.shape[2]
    seq_index = lax.axis_index("seq")
    block_view = latent_cache.reshape(local_reqs, shard_len // BLOCK, BLOCK, qk_width)
    picked = jax.vmap(pick_rows)(block_view, blocks[:, 0]).reshape(
        local_reqs, picks_count * BLOCK, qk_width
    )
    positions = (
        seq_index * shard_len + blocks[:, 0, :, None] * BLOCK + jnp.arange(BLOCK, dtype=jnp.int32)
    )
    positions = positions.reshape(local_reqs, picks_count * BLOCK)
    limits = lengths[:, None] - (drafts - 1) + jnp.arange(drafts, dtype=jnp.int32)[None, :]
    usable = positions[:, None, None, :] < limits[:, :, None, None]
    row_max, row_sum, weighted = shard_softmax(queries, picked, usable)
    row_max, row_sum, weighted = combined_all((row_max, row_sum, weighted), "seq", merge_parts)
    latent = (weighted / row_sum[..., None]).astype(jnp.bfloat16)
    head_values = jnp.einsum(
        "bqhd,hdv->bqhv", latent, value_up, preferred_element_type=jnp.float32
    ).astype(jnp.bfloat16)
    flat_values = head_values.reshape(local_reqs * drafts, head_count * DV)
    col_terms = jnp.dot(
        lax.all_gather(flat_values, "req", axis=0, tiled=True),
        out_proj,
        preferred_element_type=jnp.float32,
    )
    token_terms = lax.all_to_all(
        col_terms[None].astype(jnp.bfloat16),
        ("req", "seq", "exp"),
        split_axis=1,
        concat_axis=0,
        tiled=True,
    ).astype(jnp.float32)
    exp_count = lax.axis_size("exp")
    col_blocks = token_terms.shape[0] // exp_count
    rows_here = token_terms.shape[1]
    col_sums = jnp.sum(
        token_terms.reshape(col_blocks, exp_count, rows_here, token_terms.shape[2]), 1
    )
    attended = jnp.transpose(col_sums, (1, 0, 2)).reshape(rows_here, -1).astype(jnp.bfloat16)
    hidden_sum = (residual.astype(jnp.float32) + attended.astype(jnp.float32)).astype(jnp.bfloat16)
    hidden32 = hidden_sum.astype(jnp.float32)
    normed = (
        hidden32
        * lax.rsqrt(jnp.mean(hidden32 * hidden32, -1, keepdims=True) + 1e-06)
        * norm_gain.astype(jnp.float32)
    ).astype(jnp.bfloat16)
    gate_probs = jax.nn.sigmoid(jnp.dot(normed, router, preferred_element_type=jnp.float32))
    expert_count = router.shape[1]
    top_count = expert_ids.shape[1]
    one_hot = (expert_ids[:, :, None] == jnp.arange(expert_count, dtype=jnp.int32)).astype(
        jnp.int32
    )
    pair_hot = one_hot.reshape(rows_here * top_count, expert_count)
    slot_index = jnp.sum((jnp.cumsum(pair_hot, 0) - pair_hot) * pair_hot, -1)
    slot_hot = (slot_index[:, None] == jnp.arange(rows_here, dtype=jnp.int32)).astype(jnp.int32)
    placement = (pair_hot[:, :, None] * slot_hot[:, None, :]).reshape(
        rows_here, top_count, expert_count * rows_here
    )
    chosen = jnp.sum(one_hot.astype(jnp.float32) * gate_probs[:, None, :], -1)
    gate_weights = chosen / jnp.sum(chosen, -1, keepdims=True) * 2.5
    dispatch = jnp.sum(placement, 1).astype(jnp.bfloat16)
    outgoing = jnp.dot(dispatch.T, normed, preferred_element_type=jnp.float32).astype(jnp.bfloat16)
    outgoing = outgoing.reshape(expert_count, rows_here, outgoing.shape[1])
    combine = jnp.sum(gate_weights[:, :, None] * placement.astype(jnp.float32), 1)
    copies = lax.axis_size("seq") * exp_count
    fanned = jnp.broadcast_to(outgoing[:, None], (expert_count, copies) + outgoing.shape[1:])
    fanned = fanned.reshape((expert_count * copies,) + outgoing.shape[1:])
    returned = lax.all_to_all(
        expert_rows(
            lax.all_to_all(fanned, ("req", "seq", "exp"), split_axis=0, concat_axis=0, tiled=True),
            w_gate,
            w_up,
            w_down,
        ),
        ("req", "seq", "exp"),
        split_axis=0,
        concat_axis=0,
        tiled=True,
    )
    returned = returned.reshape((expert_count, copies) + outgoing.shape[1:]).astype(jnp.float32)
    expert_out = jnp.sum(returned, 1).astype(jnp.bfloat16)
    slot_rows = expert_out.reshape(expert_count * rows_here, expert_out.shape[2]).astype(
        jnp.float32
    )
    routed = jnp.dot(combine, slot_rows, precision=lax.Precision.HIGHEST)
    return (hidden32 + routed).astype(jnp.bfloat16)


def solution(mesh):
    in_specs = (
        P(("req", "seq", "exp"), None),
        P("req", None, "exp", None),
        P("req", "seq", None),
        P("req", "seq", None),
        P("req"),
        P("exp", None, None),
        P("exp", ("req", "seq")),
        P(),
        P(),
        P(("req", "seq", "exp"), None),
        P("req", None, ("seq", "exp")),
        P("req", None, ("seq", "exp")),
        P("req", ("seq", "exp"), None),
    )
    out_specs = P(("req", "seq", "exp"), None)
    return jax.shard_map(
        per_device, mesh=mesh, in_specs=in_specs, out_specs=out_specs, check_vma=False
    )
```

profile of v0, /device:TPU:1, one launch (start us, length us, event | category | flops | bytes accessed | tf_op | source)
XLA Modules:
  0.0 256.2 jit_solution(13494878136915248444)
XLA Ops:
  7.3 0.7 compare_select_fusion
  8.0 0.7 add_bitcast_fusion
  8.7 0.1 add.122
  8.8 0.1 copy.40
  9.0 0.2 or_reduce_fusion
  9.2 0.1 add.124
  9.3 1.5 gather_fusion
  10.9 1.5 select_reduce_fusion
  12.4 1.2 convolution_convert_fusion.2
  13.6 0.3 fusion.34
  13.9 2.9 %all-gather.2 = bf16[32,32]{1,0:T(8,128)(2,1)S(1)} all-gather(bf16[16,32]{1,0:T(8,128)(2,1)S(1)} %fusion.34), channel_id=4, replica_groups=mesh['req'=16,'seq'=2,'exp'=4] {'seq'}, dimensions={0}, use_global_device_ids=true | all-gather | bytes 3072 | tf_op jit(solution)/shard_map/all_gather | solution.py:14
  16.8 1.8 all-gather
  18.6 10.5 %all-gather.8.cloned.1.call-done = bf16[32,32,512]{2,1,0:T(8,128)(2,1)} async-done(((bf16[16,32,512]{2,1,0:T(8,128)(2,1)}), bf16[32,32,512]{2,1,0:T(8,128)(2,1)}) %all-gather.8.cloned.1.call-update) | async-done | bytes 1048592 | tf_op jit(solution)/shard_map/all_gather | solution.py:14
  29.1 1.5 fusion.22
  30.6 3.1 %fusion.15 = bf16[1,16,32,128]{3,1,2,0:T(8,128)(2,1)S(1)} fusion(bf16[32,512,128]{2,1,0:T(8,128)(2,1)} %param.18, bf16[16,32,512]{2,1,0:T(8,128)(2,1)S(1)} %fusion.22), kind=kOutput, calls=%fused_computation.18 | convolution fusion | flops 67174400 | bytes 4849664 | tf_op jit(solution)/shard_map/bqhd,hdv->bqhv/dot_general | solution.py:103
  33.8 0.7 copy.45
  34.8 0.2 select_reduce_fusion.1
  35.0 44.1 %all-gather.6.cloned.1.call-done = bf16[256,4096]{1,0:T(8,128)(2,1)} async-done(((bf16[16,4096]{1,0:T(8,128)(2,1)}), bf16[256,4096]{1,0:T(8,128)(2,1)}) %all-gather.6.cloned.1.call-update) | async-done | bytes 2097168 | tf_op jit(solution)/shard_map/all_gather | solution.py:108
  79.1 2.4 fusion.16
  81.5 0.2 copy.34
  81.7 0.5 broadcast.207
  82.2 1.5 reduce.12
  83.6 0.7 reshape.417
  84.3 9.1 %all-to-all-start = ((bf16[128,2,224]{2,1,0:T(2,128)(2,1)}), bf16[128,2,224]{2,1,0:T(2,128)(2,1)S(1)}, u32[]{:S(2)}, u32[]{:S(2)}) async-start(bf16[128,2,224]{2,1,0:T(2,128)(2,1)} %reshape.417), calls=%async_computation | async-start | bytes 262144 | tf_op jit(solution)/shard_map/all_to_all | solution.py:112
  93.4 0.1 mul.165
  93.5 0.6 reduce_sum.94
  94.2 9.3 %all-to-all-done = bf16[128,2,224]{2,1,0:T(2,128)(2,1)S(1)} async-done(((bf16[128,2,224]{2,1,0:T(2,128)(2,1)}), bf16[128,2,224]{2,1,0:T(2,128)(2,1)S(1)}, u32[]{:S(2)}, u32[]{:S(2)}) %all-to-all-start) | async-done | bytes 114720 | tf_op jit(solution)/shard_map/all_to_all | solution.py:112
  103.5 0.2 reshape.418
  103.6 0.7 bitcast_reduce_fusion.1
  104.4 0.2 reduce.7
  104.7 0.1 reshape.381
  104.8 0.2 fusion.31
  105.0 0.3 convolution_convert_fusion.1
  105.3 0.2 broadcast_in_dim.29
  105.5 1.9 broadcast_in_dim.30
  107.4 51.8 %all_to_all.19 = bf16[128,2,7168]{2,1,0:T(2,128)(2,1)} all-to-all(bf16[128,2,7168]{2,1,0:T(2,128)(2,1)S(1)} %bitcast.72), channel_id=1, replica_groups=mesh['req'=16,'seq'=2,'exp'=4] {'req','seq','exp'}, dimensions={0} | all-to-all | bytes 7340032 | tf_op jit(solution)/shard_map/all_to_all | solution.py:156
  159.2 8.4 %reshape.371 = bf16[256,7168]{1,0:T(8,128)(2,1)} reshape(bf16[128,2,7168]{2,1,0:T(2,128)(2,1)} %all_to_all.19) | data formatting | bytes 7340032 | tf_op jit(solution)/shard_map/reshape | solution.py:61
  167.6 4.3 %fusion.4 = f32[256,256]{1,0:T(8,128)S(1)} fusion(bf16[256,7168]{1,0:T(8,128)(2,1)} %reshape.371, bf16[1,7168,256]{2,1,0:T(8,128)(2,1)} %param.23), kind=kOutput, calls=%fused_computation.9 | convolution fusion | flops 939524096 | bytes 7602176 | tf_op jit(solution)/shard_map/dot_general | solution.py:62
  171.9 10.0 %convolution_convert_fusion = bf16[256,7168]{1,0:T(8,128)(2,1)} fusion(bf16[1,256,7168]{2,1,0:T(8,128)(2,1)} %param.25, bf16[256,7168]{1,0:T(8,128)(2,1)} %reshape.371, bf16[1,7168,256]{2,1,0:T(8,128)(2,1)} %param.24, f32[256,256]{1,0:T(8,128)S(1)} %fusion.4), kind=kOutput, calls=%fused_computation.1 | convolution fusion | flops 1881276416 | bytes 14942208 | tf_op jit(solution)/shard_map/dot_general | solution.py:65
  181.9 8.1 %reshape.372 = bf16[128,2,7168]{2,1,0:T(2,128)(2,1)} reshape(bf16[256,7168]{1,0:T(8,128)(2,1)} %convolution_convert_fusion) | data formatting | bytes 7340032 | tf_op jit(solution)/shard_map/reshape | solution.py:68
  190.1 4.8 %all-to-all-start.2 = ((bf16[128,2,7168]{2,1,0:T(2,128)(2,1)}), bf16[128,2,7168]{2,1,0:T(2,128)(2,1)}, u32[]{:S(2)}, u32[]{:S(2)}) async-start(bf16[128,2,7168]{2,1,0:T(2,128)(2,1)} %reshape.372), calls=%async_computation.2 | async-start | bytes 7340032 | tf_op jit(solution)/shard_map/all_to_all | solution.py:154
  194.9 0.2 fusion.19
  195.2 0.2 fusion.40
  195.4 0.1 multiply_reduce_fusion
  195.6 46.9 %all-to-all-done.2 = bf16[128,2,7168]{2,1,0:T(2,128)(2,1)} async-done(((bf16[128,2,7168]{2,1,0:T(2,128)(2,1)}), bf16[128,2,7168]{2,1,0:T(2,128)(2,1)}, u32[]{:S(2)}, u32[]{:S(2)}) %all-to-all-start.2) | async-done | bytes 3670048 | tf_op jit(solution)/shard_map/all_to_all | solution.py:154
  242.5 5.7 %bitcast_reduce_fusion = bf16[16,2,7168]{2,1,0:T(2,128)(2,1)S(1)} fusion(bf16[128,2,7168]{2,1,0:T(2,128)(2,1)} %all-to-all-done.2), kind=kLoop, calls=%fused_computation.5 | loop fusion | flops 1605632 | bytes 4128768 | tf_op jit(solution)/shard_map/reduce_sum | solution.py:167
  248.2 0.2 reshape.374
  248.4 1.0 fusion
  (35 shorter events, 0.9 us)
Async XLA Ops:
  6.5 72.5 %copy-start = (bf16[4096,224]{0,1:T(8,128)(2,1)S(1)}, bf16[4096,224]{0,1:T(8,128)(2,1)}, u32[]{:S(2)}) copy-start(bf16[4096,224]{0,1:T(8,128)(2,1)} %param.19) | copy-start | bytes 5505028
  6.5 22.6 %all-gather.8.cloned.1.call-start = ((), (), s32[]{:S(2)}) async-start(), calls=%async_computation.4 | async-start | bytes 1572864 | tf_op jit(solution)/shard_map/all_gather | solution.py:14
  13.6 65.5 %all-gather.6.cloned.1.call-start = ((), (), s32[]{:S(2)}) async-start(), calls=%async_computation.3 | async-start | bytes 2228224 | tf_op jit(solution)/shard_map/all_gather | solution.py:108
  13.6 20.9 %copy-start.3 = (s32[2,8]{1,0:T(2,128)S(1)}, s32[2,8]{1,0:T(2,128)}, u32[]{:S(2)}) copy-start(s32[2,8]{1,0:T(2,128)} %param.22) | copy-start | bytes 196
  33.7 60.4 %copy-start.2 = (bf16[7168]{0:T(1024)(128)(2,1)S(1)}, bf16[7168]{0:T(1024)(128)(2,1)}, u32[]{:S(2)}) copy-start(bf16[7168]{0:T(1024)(128)(2,1)} %param.20) | copy-start | bytes 43012
  34.5 70.3 %copy-start.1 = (bf16[2,7168]{1,0:T(2,128)(2,1)S(1)}, bf16[2,7168]{1,0:T(2,128)(2,1)}, u32[]{:S(2)}) copy-start(bf16[2,7168]{1,0:T(2,128)(2,1)} %param.13) | copy-start | bytes 86020
  84.3 19.1 %all-to-all-start = ((bf16[128,2,224]{2,1,0:T(2,128)(2,1)}), bf16[128,2,224]{2,1,0:T(2,128)(2,1)S(1)}, u32[]{:S(2)}, u32[]{:S(2)}) async-start(bf16[128,2,224]{2,1,0:T(2,128)(2,1)} %reshape.417), calls=%async_computation | async-start | bytes 262144 | tf_op jit(solution)/shard_map/all_to_all | solution.py:112
  190.1 4.8 %copy-start.4 = (bf16[7168,16]{0,1:T(8,128)(2,1)S(1)}, bf16[7168,16]{0,1:T(8,128)(2,1)}, u32[]{:S(2)}) copy-start(bf16[7168,16]{0,1:T(8,128)(2,1)} %param.21) | copy-start | bytes 688132
  190.1 52.4 %all-to-all-start.2 = ((bf16[128,2,7168]{2,1,0:T(2,128)(2,1)}), bf16[128,2,7168]{2,1,0:T(2,128)(2,1)}, u32[]{:S(2)}, u32[]{:S(2)}) async-start(bf16[128,2,7168]{2,1,0:T(2,128)(2,1)} %reshape.372), calls=%async_computation.2 | async-start | bytes 7340032 | tf_op jit(solution)/shard_map/all_to_all | solution.py:154
Sparse Core Ops, SparseCore 0:
  13.7 15.3 all-gather.7
  34.6 44.4 all-gather.5
where the time goes:
time: 257 us; the launch traced here: 256 us
  waiting for transfers between devices  111 us (43%)
  blocking collectives  56.5 us (22%)
  local copies, waits for them, and re-layouts  24.2 us (9%)
  matrix products  24 us (9%)
  between operations  14.4 us (6%)
  starting transfers between devices  13.9 us (5%)
  other arithmetic  12.3 us (5%)
    all_to_all x1, blocking collectives, per_device(): lax.all_to_all(fanned, ('req', 'seq', 'exp'), split_axis=0, concat_axis=0...  51.8 us
    all_to_all x1, waiting for transfers between devices, per_device(): lax.all_to_all(expert_rows(lax.all_to_all(fanned, ('req', 'seq', 'exp'),...  46.9 us
    all_gather x1, waiting for transfers between devices, per_device(): lax.all_gather(flat_values, 'req', axis=0, tiled=True)  44.1 us
    all_gather x1, waiting for transfers between devices, combined_all(): lax.all_gather(a.astype(kind), axis)  10.5 us
    dot_general x1, matrix products, expert_rows(): jnp.dot(activated, w_down[0], preferred_element_type=jnp.float32)  10 us
    all_to_all x1, waiting for transfers between devices, per_device(): lax.all_to_all(col_terms[None].astype(jnp.bfloat16), ('req', 'seq', 'exp'...  9.29 us
    all_to_all x1, starting transfers between devices, per_device(): lax.all_to_all(col_terms[None].astype(jnp.bfloat16), ('req', 'seq', 'exp'...  9.06 us
    reshape x1, local copies, waits for them, and re-layouts, expert_rows(): flat_rows = arrived.reshape(-1, model_width)  8.4 us
  transfers between devices with their start and end apart: 4, of which 4 were waited for; matrix products, arithmetic and copies ran while one was open for 1% of the time, Pallas kernels for 0%

commit v1 on v0

--- a/solution.py
+++ b/solution.py
@@ -2,6 +2,7 @@
 import jax.numpy as jnp
 from jax import lax
 from jax.sharding import PartitionSpec as P
+from jax.lax import all_to_all, axis_size
 
 DL = 512
 DR = 64
@@ -105,7 +106,10 @@
     ).astype(jnp.bfloat16)
     flat_values = head_values.reshape(local_reqs * drafts, head_count * DV)
     col_terms = jnp.dot(
-        lax.all_gather(flat_values, "req", axis=0, tiled=True),
+        jnp.concatenate(
+            all_to_all(jnp.stack([flat_values for _ in range(axis_size("req"))]), "req", 0, 0),
+            axis=0,
+        ),
         out_proj,
         preferred_element_type=jnp.float32,
     )

time: 257 us -> 249 us (0.969)
  waiting for transfers between devices: 111 us -> 95.6 us
  starting transfers between devices: 13.9 us -> 20.4 us
    all_gather x1 -> x0, waiting for transfers between devices: 44.1 us -> none  [per_device(): lax.all_gather(flat_values, 'req', axis=0, tiled=True)]
    all_to_all x0 -> x1, waiting for transfers between devices: none -> 28.8 us  [per_device(): all_to_all(jnp.stack([flat_values for _ in range(axis_size('req'))]), 're...]
    all_to_all x0 -> x1, starting transfers between devices: none -> 6.85 us  [per_device(): all_to_all(jnp.stack([flat_values for _ in range(axis_size('req'))]), 're...]
where the time goes in v1:
time: 249 us; the launch traced here: 248 us
  waiting for transfers between devices  95.6 us (38%)
  blocking collectives  56.5 us (23%)
  local copies, waits for them, and re-layouts  25.1 us (10%)
  matrix products  24 us (10%)
  starting transfers between devices  20.4 us (8%)
  between operations  14.5 us (6%)
  other arithmetic  12.3 us (5%)
    all_to_all x1, blocking collectives, per_device(): lax.all_to_all(fanned, ('req', 'seq', 'exp'), split_axis=0, concat_axis=0...  51.8 us
    all_to_all x1, waiting for transfers between devices, per_device(): lax.all_to_all(expert_rows(lax.all_to_all(fanned, ('req', 'seq', 'exp'),...  46.9 us
    all_to_all x1, waiting for transfers between devices, per_device(): all_to_all(jnp.stack([flat_values for _ in range(axis_size('req'))]), 're...  28.8 us
    all_gather x1, waiting for transfers between devices, combined_all(): lax.all_gather(a.astype(kind), axis)  10.6 us
    dot_general x1, matrix products, expert_rows(): jnp.dot(activated, w_down[0], preferred_element_type=jnp.float32)  10 us
    all_to_all x1, waiting for transfers between devices, per_device(): lax.all_to_all(col_terms[None].astype(jnp.bfloat16), ('req', 'seq', 'exp'...  9.29 us
    all_to_all x1, starting transfers between devices, per_device(): lax.all_to_all(col_terms[None].astype(jnp.bfloat16), ('req', 'seq', 'exp'...  8.72 us
    reshape x1, local copies, waits for them, and re-layouts, expert_rows(): flat_rows = arrived.reshape(-1, model_width)  8.4 us
  transfers between devices with their start and end apart: 4, of which 4 were waited for; matrix products, arithmetic and copies ran while one was open for 1% of the time, Pallas kernels for 0%

profile of v1, /device:TPU:1, one launch (start us, length us, event | category | flops | bytes accessed | tf_op | source)
XLA Modules:
  0.0 248.3 jit_solution(14553822227825687819)
XLA Ops:
  7.3 0.7 compare_select_fusion
  8.0 0.7 add_bitcast_fusion
  8.7 0.1 add.122
  8.8 0.1 copy.40
  9.0 0.2 or_reduce_fusion
  9.3 1.5 gather_fusion
  10.9 1.5 select_reduce_fusion
  12.4 1.2 convolution_convert_fusion.2
  13.6 0.3 fusion.34
  13.9 2.9 %all-gather.2 = bf16[32,32]{1,0:T(8,128)(2,1)S(1)} all-gather(bf16[16,32]{1,0:T(8,128)(2,1)S(1)} %fusion.34), channel_id=4, replica_groups=mesh['req'=16,'seq'=2,'exp'=4] {'seq'}, dimensions={0}, use_global_device_ids=true | all-gather | bytes 3072 | tf_op jit(solution)/shard_map/all_gather | solution.py:15
  16.7 1.8 all-gather
  18.5 10.6 %all-gather.5.cloned.1.call-done = bf16[32,32,512]{2,1,0:T(8,128)(2,1)} async-done(((bf16[16,32,512]{2,1,0:T(8,128)(2,1)}), bf16[32,32,512]{2,1,0:T(8,128)(2,1)}) %all-gather.5.cloned.1.call-update) | async-done | bytes 1048592 | tf_op jit(solution)/shard_map/all_gather | solution.py:15
  29.1 1.5 fusion.22
  30.6 3.1 %fusion.15 = bf16[1,16,32,128]{3,1,2,0:T(8,128)(2,1)S(1)} fusion(bf16[32,512,128]{2,1,0:T(8,128)(2,1)} %param.18, bf16[16,32,512]{2,1,0:T(8,128)(2,1)S(1)} %fusion.22), kind=kOutput, calls=%fused_computation.18 | convolution fusion | flops 67174400 | bytes 4849664 | tf_op jit(solution)/shard_map/bqhd,hdv->bqhv/dot_general | solution.py:104
  33.8 1.5 stack.3
  35.4 6.9 %all-to-all-start = ((bf16[16,16,4096]{2,1,0:T(8,128)(2,1)}), bf16[16,16,4096]{2,1,0:T(8,128)(2,1)}, u32[]{:S(2)}, u32[]{:S(2)}) async-start(bf16[16,16,4096]{2,1,0:T(8,128)(2,1)} %stack.3), calls=%async_computation | async-start | bytes 4194304 | tf_op jit(solution)/shard_map/all_to_all | solution.py:110
  42.5 0.2 select_reduce_fusion.1
  42.7 28.8 %all-to-all-done = bf16[16,16,4096]{2,1,0:T(8,128)(2,1)} async-done(((bf16[16,16,4096]{2,1,0:T(8,128)(2,1)}), bf16[16,16,4096]{2,1,0:T(8,128)(2,1)}, u32[]{:S(2)}, u32[]{:S(2)}) %all-to-all-start) | async-done | bytes 2097184 | tf_op jit(solution)/shard_map/all_to_all | solution.py:110
  71.5 2.4 fusion.16
  73.9 0.2 copy.34
  74.1 0.5 broadcast.208
  74.6 1.5 reduce.12
  76.0 0.7 reshape.419
  76.8 8.7 %all-to-all-start.1 = ((bf16[128,2,224]{2,1,0:T(2,128)(2,1)}), bf16[128,2,224]{2,1,0:T(2,128)(2,1)S(1)}, u32[]{:S(2)}, u32[]{:S(2)}) async-start(bf16[128,2,224]{2,1,0:T(2,128)(2,1)} %reshape.419), calls=%async_computation.1 | async-start | bytes 262144 | tf_op jit(solution)/shard_map/all_to_all | solution.py:116
  85.5 0.1 mul.165
  85.6 0.6 reduce_sum.94
  86.2 9.3 %all-to-all-done.1 = bf16[128,2,224]{2,1,0:T(2,128)(2,1)S(1)} async-done(((bf16[128,2,224]{2,1,0:T(2,128)(2,1)}), bf16[128,2,224]{2,1,0:T(2,128)(2,1)S(1)}, u32[]{:S(2)}, u32[]{:S(2)}) %all-to-all-start.1) | async-done | bytes 114720 | tf_op jit(solution)/shard_map/all_to_all | solution.py:116
  95.5 0.2 reshape.420
  95.7 0.7 bitcast_reduce_fusion.1
  96.5 0.2 reduce.7
  96.7 0.1 reshape.383
  96.9 0.2 fusion.31
  97.1 0.3 convolution_convert_fusion.1
  97.4 0.2 broadcast_in_dim.29
  97.6 1.9 broadcast_in_dim.30
  99.5 51.8 %all_to_all.24 = bf16[128,2,7168]{2,1,0:T(2,128)(2,1)} all-to-all(bf16[128,2,7168]{2,1,0:T(2,128)(2,1)S(1)} %bitcast.73), channel_id=1, replica_groups=mesh['req'=16,'seq'=2,'exp'=4] {'req','seq','exp'}, dimensions={0} | all-to-all | bytes 7340032 | tf_op jit(solution)/shard_map/all_to_all | solution.py:160
  151.3 8.4 %reshape.373 = bf16[256,7168]{1,0:T(8,128)(2,1)} reshape(bf16[128,2,7168]{2,1,0:T(2,128)(2,1)} %all_to_all.24) | data formatting | bytes 7340032 | tf_op jit(solution)/shard_map/reshape | solution.py:62
  159.7 4.3 %fusion.4 = f32[256,256]{1,0:T(8,128)S(1)} fusion(bf16[256,7168]{1,0:T(8,128)(2,1)} %reshape.373, bf16[1,7168,256]{2,1,0:T(8,128)(2,1)} %param.23), kind=kOutput, calls=%fused_computation.9 | convolution fusion | flops 939524096 | bytes 7602176 | tf_op jit(solution)/shard_map/dot_general | solution.py:63
  164.0 10.0 %convolution_convert_fusion = bf16[256,7168]{1,0:T(8,128)(2,1)} fusion(bf16[1,256,7168]{2,1,0:T(8,128)(2,1)} %param.25, bf16[256,7168]{1,0:T(8,128)(2,1)} %reshape.373, bf16[1,7168,256]{2,1,0:T(8,128)(2,1)} %param.24, f32[256,256]{1,0:T(8,128)S(1)} %fusion.4), kind=kOutput, calls=%fused_computation.1 | convolution fusion | flops 1881276416 | bytes 14942208 | tf_op jit(solution)/shard_map/dot_general | solution.py:66
  174.0 8.1 %reshape.374 = bf16[128,2,7168]{2,1,0:T(2,128)(2,1)} reshape(bf16[256,7168]{1,0:T(8,128)(2,1)} %convolution_convert_fusion) | data formatting | bytes 7340032 | tf_op jit(solution)/shard_map/reshape | solution.py:69
  182.1 4.8 %all-to-all-start.3 = ((bf16[128,2,7168]{2,1,0:T(2,128)(2,1)}), bf16[128,2,7168]{2,1,0:T(2,128)(2,1)}, u32[]{:S(2)}, u32[]{:S(2)}) async-start(bf16[128,2,7168]{2,1,0:T(2,128)(2,1)} %reshape.374), calls=%async_computation.3 | async-start | bytes 7340032 | tf_op jit(solution)/shard_map/all_to_all | solution.py:158
  187.0 0.2 fusion.19
  187.2 0.2 fusion.40
  187.5 0.1 multiply_reduce_fusion
  187.6 46.9 %all-to-all-done.3 = bf16[128,2,7168]{2,1,0:T(2,128)(2,1)} async-done(((bf16[128,2,7168]{2,1,0:T(2,128)(2,1)}), bf16[128,2,7168]{2,1,0:T(2,128)(2,1)}, u32[]{:S(2)}, u32[]{:S(2)}) %all-to-all-start.3) | async-done | bytes 3670048 | tf_op jit(solution)/shard_map/all_to_all | solution.py:158
  234.6 5.7 %bitcast_reduce_fusion = bf16[16,2,7168]{2,1,0:T(2,128)(2,1)S(1)} fusion(bf16[128,2,7168]{2,1,0:T(2,128)(2,1)} %all-to-all-done.3), kind=kLoop, calls=%fused_computation.5 | loop fusion | flops 1605632 | bytes 4128768 | tf_op jit(solution)/shard_map/reduce_sum | solution.py:171
  240.3 0.2 reshape.376
  240.5 1.0 fusion
  (35 shorter events, 1.0 us)
Async XLA Ops:
  6.5 65.0 %copy-start = (bf16[4096,224]{0,1:T(8,128)(2,1)S(1)}, bf16[4096,224]{0,1:T(8,128)(2,1)}, u32[]{:S(2)}) copy-start(bf16[4096,224]{0,1:T(8,128)(2,1)} %param.19) | copy-start | bytes 5505028
  6.5 22.6 %all-gather.5.cloned.1.call-start = ((), (), s32[]{:S(2)}) async-start(), calls=%async_computation.4 | async-start | bytes 1572864 | tf_op jit(solution)/shard_map/all_gather | solution.py:15
  33.7 8.5 %copy-start.3 = (s32[2,8]{1,0:T(2,128)S(1)}, s32[2,8]{1,0:T(2,128)}, u32[]{:S(2)}) copy-start(s32[2,8]{1,0:T(2,128)} %param.22) | copy-start | bytes 196
  35.4 36.1 %all-to-all-start = ((bf16[16,16,4096]{2,1,0:T(8,128)(2,1)}), bf16[16,16,4096]{2,1,0:T(8,128)(2,1)}, u32[]{:S(2)}, u32[]{:S(2)}) async-start(bf16[16,16,4096]{2,1,0:T(8,128)(2,1)} %stack.3), calls=%async_computation | async-start | bytes 4194304 | tf_op jit(solution)/shard_map/all_to_all | solution.py:110
  42.2 44.0 %copy-start.2 = (bf16[7168]{0:T(1024)(128)(2,1)S(1)}, bf16[7168]{0:T(1024)(128)(2,1)}, u32[]{:S(2)}) copy-start(bf16[7168]{0:T(1024)(128)(2,1)} %param.20) | copy-start | bytes 43012
  42.3 54.6 %copy-start.1 = (bf16[2,7168]{1,0:T(2,128)(2,1)S(1)}, bf16[2,7168]{1,0:T(2,128)(2,1)}, u32[]{:S(2)}) copy-start(bf16[2,7168]{1,0:T(2,128)(2,1)} %param.13) | copy-start | bytes 86020
  76.8 18.8 %all-to-all-start.1 = ((bf16[128,2,224]{2,1,0:T(2,128)(2,1)}), bf16[128,2,224]{2,1,0:T(2,128)(2,1)S(1)}, u32[]{:S(2)}, u32[]{:S(2)}) async-start(bf16[128,2,224]{2,1,0:T(2,128)(2,1)} %reshape.419), calls=%async_computation.1 | async-start | bytes 262144 | tf_op jit(solution)/shard_map/all_to_all | solution.py:116
  182.1 4.8 %copy-start.4 = (bf16[7168,16]{0,1:T(8,128)(2,1)S(1)}, bf16[7168,16]{0,1:T(8,128)(2,1)}, u32[]{:S(2)}) copy-start(bf16[7168,16]{0,1:T(8,128)(2,1)} %param.21) | copy-start | bytes 688132
  182.1 52.4 %all-to-all-start.3 = ((bf16[128,2,7168]{2,1,0:T(2,128)(2,1)}), bf16[128,2,7168]{2,1,0:T(2,128)(2,1)}, u32[]{:S(2)}, u32[]{:S(2)}) async-start(bf16[128,2,7168]{2,1,0:T(2,128)(2,1)} %reshape.374), calls=%async_computation.3 | async-start | bytes 7340032 | tf_op jit(solution)/shard_map/all_to_all | solution.py:158
Sparse Core Ops, SparseCore 0:
  13.7 15.3 all-gather.4
